TPU v7x, 32 devices: a whole 2x2x4 slice. The times are simulated.
32 devices in a mesh: inst: 4 (over z), shard: 8 (over y, x, core).
Axes of the slice: x: 2, y: 2, z: 4, core: 2. Of those that a mesh axis runs over, the one named last changes fastest.
Arguments:
- master_old: float32 [4, 16, 65536], P('inst', 'shard'), may hold values from -3 to 3
- first_old: float32 [4, 16, 65536], P('inst', 'shard'), may hold values from -2 to 2
- second_old: float32 [4, 16, 65536], P('inst', 'shard'), may hold values from 0.01 to 1
- healthy: int32 [8], replicated, may hold values from 0 to 3
- slice_table: int32 [16], replicated, may hold values from 0 to 15, as said below
Outputs:
- master_new: float32 [4, 16, 65536], P('inst', 'shard')
- first_new: float32 [4, 16, 65536], P('inst', 'shard')
- second_new: float32 [4, 16, 65536], P('inst', 'shard')
- params_half: bfloat16 [4, 16, 65536], P('inst', 'shard')
- checksum: float32 [4, 2], P('inst')
Inputs may be any that keep to these rules, and one draw needn't show every extreme that they name: slice_table[k] = (k + slice_table[0]) mod 16 for every k, with slice_table[0] odd and at least 3.
All inputs are finite; a program needn't handle non-finite values.
Results may differ from a plain program's by a relative error of at most 0.001.
Values sent between devices are 32-bit elements; how exact they have to be, the bound alone decides.
No kernel may reach another device: no remote copies, remote signals or barrier semaphores. Data moves between devices by JAX's collectives and lax.ppermute only.
A program may use at most 64 MiB of HBM per device.

v0:
```python
import jax
import jax.numpy as jnp
from jax import lax
from jax.sharding import PartitionSpec as P


def passed_along(value, axis, steps):
    count = lax.axis_size(axis)
    pairs = [(source, (source + steps) % count) for source in range(count)]
    return lax.ppermute(value, axis, pairs)


def from_root(block, axis, owner):
    block = jnp.where(lax.axis_index(axis) == owner, block, jnp.zeros_like(block))
    return lax.psum(block, axis)


def position_keys(flat_rows, columns):
    residue = flat_rows * (columns % 101) % 101
    offsets = jnp.arange(columns, dtype=jnp.int32)
    cycled = (residue[:, None] + offsets[None, :]) % 101
    return (cycled * 37 % 101 + 1).astype(jnp.float32) / 101.0


def weighted(master, first_moment, second, flat_rows):
    weights = position_keys(flat_rows, master.shape[2])
    combined = master[0] + first_moment[0] + second[0]
    return jnp.stack([jnp.sum(combined * weights), jnp.sum(master[0] * weights)])


def grand_total(partial_value):
    return lax.psum(partial_value, "shard")


def join_parts(pieces):
    return (
        lax.all_gather(pieces[0], "inst", axis=2, tiled=True),
        lax.all_gather(pieces[1], "inst", axis=2, tiled=True),
        lax.all_gather(pieces[2], "inst", axis=2, tiled=True),
    )


def reorder(arrays, rotation, owners):
    for bit_level in range((owners - 1).bit_length()):
        shifted = passed_along((arrays[0], arrays[1], arrays[2]), "shard", 1 << bit_level)
        chosen = rotation >> bit_level & 1 == 1
        arrays = tuple(
            (
                jnp.where(chosen, shifted_one, current)
                for shifted_one, current in zip(shifted, arrays)
            )
        )
    carried = passed_along((arrays[0][:, 1:2], arrays[1][:, 1:2], arrays[2][:, 1:2]), "shard", 1)
    return tuple(
        (
            jnp.concatenate([carried_one, current[:, 0:1]], axis=1)
            for carried_one, current in zip(carried, arrays)
        )
    )


def on_device(master_old, first_old, second_old, healthy, slice_table):
    source_index = lax.dynamic_index_in_dim(healthy, lax.axis_index("shard"), 0, keepdims=False)
    owners = lax.axis_size("shard")
    instances = lax.axis_size("inst")
    columns = master_old.shape[2]
    part_len = columns // instances
    normalizer = 1.0 / (2.0 * columns)
    rotation = slice_table[0] // 2
    master, first_moment, second = (
        from_root(master_old, "inst", source_index),
        from_root(first_old, "inst", source_index),
        from_root(second_old, "inst", source_index),
    )
    offset_start = lax.axis_index("inst") * part_len
    pieces = tuple(
        (
            lax.dynamic_slice_in_dim(stacked, offset_start, part_len, 2)
            for stacked in (master, first_moment, second)
        )
    )
    pieces = reorder(pieces, rotation, owners)
    master, first_moment, second = join_parts(pieces)
    new_rows = 2 * lax.axis_index("shard") + jnp.arange(2, dtype=jnp.int32)
    checksum = grand_total(weighted(master, first_moment, second, new_rows))
    checksum = jnp.reshape(checksum * normalizer, (1, 2))
    return (master, first_moment, second, master.astype(jnp.bfloat16), checksum)


def solution(mesh):
    placed = (
        P("inst", "shard", None),
        P("inst", "shard", None),
        P("inst", "shard", None),
        P(),
        P(),
    )
    return jax.shard_map(
        on_device,
        mesh=mesh,
        in_specs=placed,
        out_specs=(
            P("inst", "shard", None),
            P("inst", "shard", None),
            P("inst", "shard", None),
            P("inst", "shard", None),
            P("inst", None),
        ),
        check_vma=False,
    )
```

profile of v0, /device:TPU:0, one launch (start us, length us, event | category | flops | bytes accessed | tf_op | source)
XLA Modules:
  0.0 187.4 jit_solution(15723886663687752897)
XLA Ops:
  9.1 2.1 %broadcast_select_fusion.2 = f32[1,2,65536]{2,1,0:T(2,128)} fusion(f32[1,2,65536]{2,1,0:T(2,128)} %param.5, pred[]{:T(512)S(6)} %eq.22), kind=kLoop, calls=%fused_computation.15 | loop fusion | flops 131072 | bytes 1048577 | tf_op jit(solution)/shard_map/jit(_where)/select_n | solution.py:14
  11.3 1.5 broadcast_select_fusion
  13.7 70.2 %all-reduce.3.cloned.1.call-done = (f32[1,2,65536]{2,1,0:T(2,128)}, f32[1,2,65536]{2,1,0:T(2,128)}, f32[1,2,65536]{2,1,0:T(2,128)}) async-done(((f32[1,2,65536]{2,1,0:T(2,128)}, f32[1,2,65536]{2,1,0:T(2,128)}, f32[1,2,65536]{2,1,0:T(2,128)}), (f32[1,2,65536]{2,1,0:T(2,128)}, f32[1,2,65536]{2,1,0:T(2,128)}, f32[1,2,65536]{2,1,0:T(2,128)})) %all-reduce.3.cloned.1.call-update) | async-done | bytes 1572880 | tf_op jit(solution)/shard_map/psum | solution.py:15
  83.9 1.0 constant_dynamic-slice_fusion
  84.9 0.9 constant_dynamic-slice_fusion.1
  85.8 1.6 collective-permute-start.4
  87.6 2.6 %collective-permute-done.8 = f32[1,2,16384]{2,1,0:T(2,128)S(1)} collective-permute-done((f32[1,2,16384]{2,1,0:T(2,128)S(1)}, f32[1,2,16384]{2,1,0:T(2,128)S(1)}, u32[]{:S(2)}, u32[]{:S(2)}) %collective-permute-start.8) | collective-permute-done | bytes 131104 | tf_op jit(solution)/shard_map/ppermute | solution.py:10
  90.2 1.0 broadcast_select_fusion.3
  91.8 1.0 broadcast_select_fusion.4
  92.8 2.4 %collective-permute-start.5 = (f32[1,2,16384]{2,1,0:T(2,128)S(1)}, f32[1,2,16384]{2,1,0:T(2,128)S(1)}, u32[]{:S(2)}, u32[]{:S(2)}) collective-permute-start(f32[1,2,16384]{2,1,0:T(2,128)S(1)} %broadcast_select_fusion.4), channel_id=1, source_target_pairs={{0,2},{1,3},{2,4},{3,5},{4,6},{5,7},{6,0},{7,1},{8,10},{9,11},{10,... | collective-permute-start | bytes 393224 | tf_op jit(solution)/shard_map/ppermute | solution.py:10
  95.9 2.5 %collective-permute-done.9 = f32[1,2,16384]{2,1,0:T(2,128)S(1)} collective-permute-done((f32[1,2,16384]{2,1,0:T(2,128)S(1)}, f32[1,2,16384]{2,1,0:T(2,128)S(1)}, u32[]{:S(2)}, u32[]{:S(2)}) %collective-permute-start.9) | collective-permute-done | bytes 131104 | tf_op jit(solution)/shard_map/ppermute | solution.py:10
  98.5 1.7 collective-permute-start.10
  100.2 1.0 collective-permute-done.5
  101.3 1.0 collective-permute-start.6
  103.7 1.9 %collective-permute-done.10 = f32[1,2,16384]{2,1,0:T(2,128)S(1)} collective-permute-done((f32[1,2,16384]{2,1,0:T(2,128)S(1)}, f32[1,2,16384]{2,1,0:T(2,128)S(1)}, u32[]{:S(2)}, u32[]{:S(2)}) %collective-permute-start.10) | collective-permute-done | bytes 131104 | tf_op jit(solution)/shard_map/ppermute | solution.py:10
  105.9 2.6 %collective-permute-done.6 = f32[1,2,16384]{2,1,0:T(2,128)S(1)} collective-permute-done((f32[1,2,16384]{2,1,0:T(2,128)S(1)}, f32[1,2,16384]{2,1,0:T(2,128)S(1)}, u32[]{:S(2)}, u32[]{:S(2)}) %collective-permute-start.6) | collective-permute-done | bytes 131104 | tf_op jit(solution)/shard_map/ppermute | solution.py:10
  108.7 3.2 %collective-permute-done.2 = f32[1,2,16384]{2,1,0:T(2,128)S(1)} collective-permute-done((f32[1,2,16384]{2,1,0:T(2,128)S(1)}, f32[1,2,16384]{2,1,0:T(2,128)S(1)}, u32[]{:S(2)}, u32[]{:S(2)}) %collective-permute-start.2) | collective-permute-done | bytes 131104 | tf_op jit(solution)/shard_map/ppermute | solution.py:10
  112.2 16.1 %all_gather.11 = f32[1,2,65536]{2,1,0:T(2,128)S(1)} all-gather(f32[1,2,16384]{2,1,0:T(2,128)S(1)} %pad_maximum_fusion.2), channel_id=1, replica_groups=mesh['inst'=4,'shard'=8] {'inst'}, dimensions={2}, use_global_device_ids=true | all-gather | bytes 655360 | tf_op jit(solution)/shard_map/all_gather | solution.py:39
  128.4 15.8 %all_gather.10 = f32[1,2,65536]{2,1,0:T(2,128)S(1)} all-gather(f32[1,2,16384]{2,1,0:T(2,128)S(1)} %pad_maximum_fusion.1), channel_id=1, replica_groups=mesh['inst'=4,'shard'=8] {'inst'}, dimensions={2}, use_global_device_ids=true | all-gather | bytes 655360 | tf_op jit(solution)/shard_map/all_gather | solution.py:38
  144.3 15.0 %all_gather.9 = f32[1,2,65536]{2,1,0:T(2,128)S(1)} all-gather(f32[1,2,16384]{2,1,0:T(2,128)S(1)} %pad_maximum_fusion), channel_id=1, replica_groups=mesh['inst'=4,'shard'=8] {'inst'}, dimensions={2}, use_global_device_ids=true | all-gather | bytes 655360 | tf_op jit(solution)/shard_map/all_gather | solution.py:37
  159.3 4.3 %fusion.6 = (f32[]{:T(128)}, f32[]{:T(128)}) fusion(f32[1,2,65536]{2,1,0:T(2,128)S(1)} %all_gather.11, f32[1,2,65536]{2,1,0:T(2,128)S(1)} %all_gather.10, f32[1,2,65536]{2,1,0:T(2,128)S(1)} %all_gather.9, s32[2]{0:T(128)S(1)} %and_select_fusion.2), kind=kLoop, calls=%fused_computation.9 | loop fusion | flops 3014654 | bytes 1572880 | tf_op jit(solution)/shard_map/reduce_sum | solution.py:28
  163.6 1.4 pad_maximum_fusion.3
  165.0 0.9 convert_element_type.6
  165.9 11.8 %psum.31 = f32[2]{0:T(128)S(1)} all-reduce(f32[2]{0:T(128)S(1)} %pad_maximum_fusion.3), channel_id=1, replica_groups=mesh['inst'=4,'shard'=8] {'shard'}, use_global_device_ids=true, to_apply=%region_5.6 | all-reduce | flops 2 | bytes 16 | tf_op jit(solution)/shard_map/psum | solution.py:32
  (46 shorter events, 8.9 us)
Async XLA Ops:
  7.2 76.7 %all-reduce.3.cloned.1.call-start = ((), (), s32[]{:S(2)}) async-start(), calls=%async_computation | async-start | bytes 3145728 | tf_op jit(solution)/shard_map/psum | solution.py:15
  7.2 0.7 copy-start.4
  9.1 2.2 %copy-start = (f32[1,2,65536]{2,1,0:T(2,128)S(1)}, f32[1,2,65536]{2,1,0:T(2,128)}, u32[]{:S(2)}) copy-start(f32[1,2,65536]{2,1,0:T(2,128)} %param.7) | copy-start | bytes 1572868
  9.1 2.2 %copy-start.1 = (f32[1,2,65536]{2,1,0:T(2,128)S(1)}, f32[1,2,65536]{2,1,0:T(2,128)}, u32[]{:S(2)}) copy-start(f32[1,2,65536]{2,1,0:T(2,128)} %param.6) | copy-start | bytes 1572868
  12.8 0.7 copy-start.3
  83.9 3.6 %copy-start.2 = (f32[1,2,65536]{2,1,0:T(2,128)S(1)}, f32[1,2,65536]{2,1,0:T(2,128)}, u32[]{:S(2)}) copy-start(f32[1,2,65536]{2,1,0:T(2,128)} %get-tuple-element.7) | copy-start | bytes 1572868
  84.9 5.3 %collective-permute-start.8 = (f32[1,2,16384]{2,1,0:T(2,128)S(1)}, f32[1,2,16384]{2,1,0:T(2,128)S(1)}, u32[]{:S(2)}, u32[]{:S(2)}) collective-permute-start(f32[1,2,16384]{2,1,0:T(2,128)S(1)} %constant_dynamic-slice_fusion), channel_id=1, source_target_pairs={{0,1},{1,2},{2,3},{3,4},{4,5},{5,6},{6,7},{7,0},{8,9},{9,10},{10,1... | collective-permute-start | bytes 393224 | tf_op jit(solution)/shard_map/ppermute | solution.py:10
  85.8 6.0 %collective-permute-start.4 = (f32[1,2,16384]{2,1,0:T(2,128)S(1)}, f32[1,2,16384]{2,1,0:T(2,128)S(1)}, u32[]{:S(2)}, u32[]{:S(2)}) collective-permute-start(f32[1,2,16384]{2,1,0:T(2,128)S(1)} %constant_dynamic-slice_fusion.1), channel_id=1, source_target_pairs={{0,1},{1,2},{2,3},{3,4},{4,5},{5,6},{6,7},{7,0},{8,9},{9,10},{10,1... | collective-permute-start | bytes 393224 | tf_op jit(solution)/shard_map/ppermute | solution.py:10
  87.5 7.7 %collective-permute-start = (f32[1,2,16384]{2,1,0:T(2,128)S(1)}, f32[1,2,16384]{2,1,0:T(2,128)S(1)}, u32[]{:S(2)}, u32[]{:S(2)}) collective-permute-start(f32[1,2,16384]{2,1,0:T(2,128)S(1)} %constant_dynamic-slice_fusion.2), channel_id=1, source_target_pairs={{0,1},{1,2},{2,3},{3,4},{4,5},{5,6},{6,7},{7,0},{8,9},{9,10},{10,1... | collective-permute-start | bytes 393224 | tf_op jit(solution)/shard_map/ppermute | solution.py:10
  91.2 7.2 %collective-permute-start.9 = (f32[1,2,16384]{2,1,0:T(2,128)S(1)}, f32[1,2,16384]{2,1,0:T(2,128)S(1)}, u32[]{:S(2)}, u32[]{:S(2)}) collective-permute-start(f32[1,2,16384]{2,1,0:T(2,128)S(1)} %broadcast_select_fusion.3), channel_id=1, source_target_pairs={{0,2},{1,3},{2,4},{3,5},{4,6},{5,7},{6,0},{7,1},{8,10},{9,11},{10,... | collective-permute-start | bytes 393224 | tf_op jit(solution)/shard_map/ppermute | solution.py:10
  92.8 8.5 %collective-permute-start.5 = (f32[1,2,16384]{2,1,0:T(2,128)S(1)}, f32[1,2,16384]{2,1,0:T(2,128)S(1)}, u32[]{:S(2)}, u32[]{:S(2)}) collective-permute-start(f32[1,2,16384]{2,1,0:T(2,128)S(1)} %broadcast_select_fusion.4), channel_id=1, source_target_pairs={{0,2},{1,3},{2,4},{3,5},{4,6},{5,7},{6,0},{7,1},{8,10},{9,11},{10,... | collective-permute-start | bytes 393224 | tf_op jit(solution)/shard_map/ppermute | solution.py:10
  95.3 7.5 %collective-permute-start.1 = (f32[1,2,16384]{2,1,0:T(2,128)S(1)}, f32[1,2,16384]{2,1,0:T(2,128)S(1)}, u32[]{:S(2)}, u32[]{:S(2)}) collective-permute-start(f32[1,2,16384]{2,1,0:T(2,128)S(1)} %broadcast_select_fusion.5), channel_id=1, source_target_pairs={{0,2},{1,3},{2,4},{3,5},{4,6},{5,7},{6,0},{7,1},{8,10},{9,11},{10,... | collective-permute-start | bytes 393224 | tf_op jit(solution)/shard_map/ppermute | solution.py:10
  98.5 7.1 %collective-permute-start.10 = (f32[1,2,16384]{2,1,0:T(2,128)S(1)}, f32[1,2,16384]{2,1,0:T(2,128)S(1)}, u32[]{:S(2)}, u32[]{:S(2)}) collective-permute-start(f32[1,2,16384]{2,1,0:T(2,128)S(1)} %broadcast_select_fusion.6), channel_id=1, source_target_pairs={{0,4},{1,5},{2,6},{3,7},{4,0},{5,1},{6,2},{7,3},{8,12},{9,13},{10,... | collective-permute-start | bytes 393224 | tf_op jit(solution)/shard_map/ppermute | solution.py:10
  101.3 7.1 %collective-permute-start.6 = (f32[1,2,16384]{2,1,0:T(2,128)S(1)}, f32[1,2,16384]{2,1,0:T(2,128)S(1)}, u32[]{:S(2)}, u32[]{:S(2)}) collective-permute-start(f32[1,2,16384]{2,1,0:T(2,128)S(1)} %broadcast_select_fusion.7), channel_id=1, source_target_pairs={{0,4},{1,5},{2,6},{3,7},{4,0},{5,1},{6,2},{7,3},{8,12},{9,13},{10,... | collective-permute-start | bytes 393224 | tf_op jit(solution)/shard_map/ppermute | solution.py:10
  102.9 9.0 %collective-permute-start.2 = (f32[1,2,16384]{2,1,0:T(2,128)S(1)}, f32[1,2,16384]{2,1,0:T(2,128)S(1)}, u32[]{:S(2)}, u32[]{:S(2)}) collective-permute-start(f32[1,2,16384]{2,1,0:T(2,128)S(1)} %broadcast_select_fusion.8), channel_id=1, source_target_pairs={{0,4},{1,5},{2,6},{3,7},{4,0},{5,1},{6,2},{7,3},{8,12},{9,13},{10,... | collective-permute-start | bytes 393224 | tf_op jit(solution)/shard_map/ppermute | solution.py:10
  105.8 6.3 %collective-permute-start.11 = (f32[1,1,16384]{2,1,0:T(1,128)S(1)}, f32[1,1,16384]{2,1,0:T(1,128)S(1)}, u32[]{:S(2)}, u32[]{:S(2)}) collective-permute-start(f32[1,1,16384]{2,1,0:T(1,128)S(1)} %get-tuple-element.10), channel_id=1, source_target_pairs={{0,1},{1,2},{2,3},{3,4},{4,5},{5,6},{6,7},{7,0},{8,9},{9,10},{10,1... | collective-permute-start | bytes 196616 | tf_op jit(solution)/shard_map/ppermute | solution.py:10
  108.6 19.7 %collective-permute-start.7 = (f32[1,1,16384]{2,1,0:T(1,128)S(1)}, f32[1,1,16384]{2,1,0:T(1,128)S(1)}, u32[]{:S(2)}, u32[]{:S(2)}) collective-permute-start(f32[1,1,16384]{2,1,0:T(1,128)S(1)} %get-tuple-element.12), channel_id=1, source_target_pairs={{0,1},{1,2},{2,3},{3,4},{4,5},{5,6},{6,7},{7,0},{8,9},{9,10},{10,1... | collective-permute-start | bytes 196616 | tf_op jit(solution)/shard_map/ppermute | solution.py:10
  112.0 32.2 %collective-permute-start.3 = (f32[1,1,16384]{2,1,0:T(1,128)S(1)}, f32[1,1,16384]{2,1,0:T(1,128)S(1)}, u32[]{:S(2)}, u32[]{:S(2)}) collective-permute-start(f32[1,1,16384]{2,1,0:T(1,128)S(1)} %get-tuple-element.14), channel_id=1, source_target_pairs={{0,1},{1,2},{2,3},{3,4},{4,5},{5,6},{6,7},{7,0},{8,9},{9,10},{10,1... | collective-permute-start | bytes 196616 | tf_op jit(solution)/shard_map/ppermute | solution.py:10
Sparse Core Ops, SparseCore 0:
  12.9 70.8 all-reduce.2
where the time goes:
time: 188 us; the launch traced here: 187 us
  waiting for transfers between devices  84.6 us (45%)
  blocking collectives  58.6 us (31%)
  between operations  15 us (8%)
  other arithmetic  13.5 us (7%)
  starting transfers between devices  9.11 us (5%)
  local copies, waits for them, and re-layouts  6.49 us (3%)
    psum x1, waiting for transfers between devices, from_root(): return lax.psum(block, axis)  70.2 us
    all_gather x1, blocking collectives, join_parts(): lax.all_gather(pieces[2], 'inst', axis=2, tiled=True)  16.1 us
    all_gather x1, blocking collectives, join_parts(): lax.all_gather(pieces[1], 'inst', axis=2, tiled=True)  15.8 us
    all_gather x1, blocking collectives, join_parts(): lax.all_gather(pieces[0], 'inst', axis=2, tiled=True)  15 us
    ppermute x12, waiting for transfers between devices, passed_along(): return lax.ppermute(value, axis, pairs)  14.4 us
    psum x1, blocking collectives, grand_total(): return lax.psum(partial_value, 'shard')  11.8 us
    ppermute x12, starting transfers between devices, passed_along(): return lax.ppermute(value, axis, pairs)  9.07 us
    reduce_sum x1, other arithmetic, weighted(): jnp.sum(combined * weights)  4.28 us
  transfers between devices with their start and end apart: 13, of which 8 were waited for; matrix products, arithmetic and copies ran while one was open for 2% of the time, Pallas kernels for 0%

commit v1 on v0

--- a/solution.py
+++ b/solution.py
@@ -2,6 +2,23 @@
 import jax.numpy as jnp
 from jax import lax
 from jax.sharding import PartitionSpec as P
+
+
+def laid_out(parts, dim):
+    shape = list(parts.shape[1:])
+    shape[dim] *= parts.shape[0]
+    return jnp.moveaxis(parts, 0, dim).reshape(shape)
+
+
+def gather_around(value, axis, dim):
+    size = lax.axis_size(axis)
+    upward = [(i, (i + 1) % size) for i in range(size)]
+    blocks = [value]
+    while len(blocks) < size:
+        blocks.append(lax.ppermute(blocks[-1], axis, upward))
+    mine = lax.axis_index(axis)
+    blocks = jnp.stack(blocks)[(mine - jnp.arange(size)) % size]
+    return laid_out(blocks, dim)
 
 
 def passed_along(value, axis, steps):
@@ -34,7 +51,7 @@
 
 def join_parts(pieces):
     return (
-        lax.all_gather(pieces[0], "inst", axis=2, tiled=True),
+        gather_around(pieces[0], "inst", 2),
         lax.all_gather(pieces[1], "inst", axis=2, tiled=True),
         lax.all_gather(pieces[2], "inst", axis=2, tiled=True),
     )

time: 188 us -> 187 us (level)
  blocking collectives: 58.6 us -> 45.3 us
  waiting for transfers between devices: 84.6 us -> 90.7 us
  other arithmetic: 13.5 us -> 17.5 us
  starting transfers between devices: 9.11 us -> 11.2 us
    all_gather x1 -> x0, blocking collectives: 15 us -> none  [join_parts(): lax.all_gather(pieces[0], 'inst', axis=2, tiled=True)]
    reduce_sum x0 -> x1, other arithmetic: none -> 3.9 us  [weighted(): jnp.sum(master[0] * weights)]
    ppermute x12, waiting for transfers between devices: 14.4 us -> 17.8 us  [passed_along(): return lax.ppermute(value, axis, pairs)]
    ppermute x0 -> x3, waiting for transfers between devices: none -> 2.73 us  [gather_around(): blocks.append(lax.ppermute(blocks[-1], axis, upward))]
    ppermute x0 -> x3, starting transfers between devices: none -> 2.06 us  [gather_around(): blocks.append(lax.ppermute(blocks[-1], axis, upward))]
  transfers between devices with their start and end apart: 13 -> 16, of which waited for: 8 -> 11; matrix products, arithmetic and copies ran while one was open for 2% -> 2% of each run, Pallas kernels for 0% -> 0%
where the time goes in v1:
time: 187 us
  waiting for transfers between devices  90.7 us (49%)
  blocking collectives  45.3 us (24%)
  other arithmetic  17.5 us (9%)
  between operations  15.1 us (8%)
  starting transfers between devices  11.2 us (6%)
  local copies, waits for them, and re-layouts  6.81 us (4%)
    psum x1, waiting for transfers between devices, from_root(): return lax.psum(block, axis)  70.1 us
    ppermute x12, waiting for transfers between devices, passed_along(): return lax.ppermute(value, axis, pairs)  17.8 us
    all_gather x1, blocking collectives, join_parts(): lax.all_gather(pieces[1], 'inst', axis=2, tiled=True)  17.2 us
    all_gather x1, blocking collectives, join_parts(): lax.all_gather(pieces[2], 'inst', axis=2, tiled=True)  16.3 us
    psum x1, blocking collectives, grand_total(): return lax.psum(partial_value, 'shard')  11.8 us
    ppermute x12, starting transfers between devices, passed_along(): return lax.ppermute(value, axis, pairs)  9.07 us
    reduce_sum x1, other arithmetic, weighted(): jnp.sum(combined * weights)  4.08 us
    reduce_sum x1, other arithmetic, weighted(): jnp.sum(master[0] * weights)  3.9 us
  transfers between devices with their start and end apart: 16, of which 11 were waited for; matrix products, arithmetic and copies ran while one was open for 2% of the time, Pallas kernels for 0%

profile of v1, /device:TPU:0, one launch (start us, length us, event | category | flops | bytes accessed | tf_op | source)
XLA Modules:
  0.0 186.5 jit_solution(12155491193941504130)
XLA Ops:
  9.1 2.2 %broadcast_select_fusion.2 = f32[1,2,65536]{2,1,0:T(2,128)} fusion(f32[1,2,65536]{2,1,0:T(2,128)} %param.5, pred[]{:T(512)S(6)} %eq.24), kind=kLoop, calls=%fused_computation.23 | loop fusion | flops 131072 | bytes 1048577 | tf_op jit(solution)/shard_map/jit(_where)/select_n | solution.py:31
  11.3 1.5 broadcast_select_fusion
  13.8 70.1 %all-reduce.3.cloned.1.call-done = (f32[1,2,65536]{2,1,0:T(2,128)}, f32[1,2,65536]{2,1,0:T(2,128)}, f32[1,2,65536]{2,1,0:T(2,128)}) async-done(((f32[1,2,65536]{2,1,0:T(2,128)}, f32[1,2,65536]{2,1,0:T(2,128)}, f32[1,2,65536]{2,1,0:T(2,128)}), (f32[1,2,65536]{2,1,0:T(2,128)}, f32[1,2,65536]{2,1,0:T(2,128)}, f32[1,2,65536]{2,1,0:T(2,128)})) %all-reduce.3.cloned.1.call-update) | async-done | bytes 1572880 | tf_op jit(solution)/shard_map/psum | solution.py:32
  85.8 1.6 collective-permute-start.7
  87.6 2.6 %collective-permute-done = f32[1,2,16384]{2,1,0:T(2,128)S(1)} collective-permute-done((f32[1,2,16384]{2,1,0:T(2,128)S(1)}, f32[1,2,16384]{2,1,0:T(2,128)S(1)}, u32[]{:S(2)}, u32[]{:S(2)}) %collective-permute-start) | collective-permute-done | bytes 131104 | tf_op jit(solution)/shard_map/ppermute | solution.py:27
  90.2 1.0 broadcast_select_fusion.5
  91.8 1.0 broadcast_select_fusion.4
  92.8 2.4 %collective-permute-start.8 = (f32[1,2,16384]{2,1,0:T(2,128)S(1)}, f32[1,2,16384]{2,1,0:T(2,128)S(1)}, u32[]{:S(2)}, u32[]{:S(2)}) collective-permute-start(f32[1,2,16384]{2,1,0:T(2,128)S(1)} %broadcast_select_fusion.4), channel_id=1, source_target_pairs={{0,2},{1,3},{2,4},{3,5},{4,6},{5,7},{6,0},{7,1},{8,10},{9,11},{10,... | collective-permute-start | bytes 393224 | tf_op jit(solution)/shard_map/ppermute | solution.py:27
  95.9 2.5 %collective-permute-done.1 = f32[1,2,16384]{2,1,0:T(2,128)S(1)} collective-permute-done((f32[1,2,16384]{2,1,0:T(2,128)S(1)}, f32[1,2,16384]{2,1,0:T(2,128)S(1)}, u32[]{:S(2)}, u32[]{:S(2)}) %collective-permute-start.1) | collective-permute-done | bytes 131104 | tf_op jit(solution)/shard_map/ppermute | solution.py:27
  98.5 1.7 collective-permute-start.2
  100.2 1.0 collective-permute-done.8
  103.7 1.9 %collective-permute-done.2 = f32[1,2,16384]{2,1,0:T(2,128)S(1)} collective-permute-done((f32[1,2,16384]{2,1,0:T(2,128)S(1)}, f32[1,2,16384]{2,1,0:T(2,128)S(1)}, u32[]{:S(2)}, u32[]{:S(2)}) %collective-permute-start.2) | collective-permute-done | bytes 131104 | tf_op jit(solution)/shard_map/ppermute | solution.py:27
  105.9 2.6 %collective-permute-done.9 = f32[1,2,16384]{2,1,0:T(2,128)S(1)} collective-permute-done((f32[1,2,16384]{2,1,0:T(2,128)S(1)}, f32[1,2,16384]{2,1,0:T(2,128)S(1)}, u32[]{:S(2)}, u32[]{:S(2)}) %collective-permute-start.9) | collective-permute-done | bytes 131104 | tf_op jit(solution)/shard_map/ppermute | solution.py:27
  108.7 3.2 %collective-permute-done.13 = f32[1,2,16384]{2,1,0:T(2,128)S(1)} collective-permute-done((f32[1,2,16384]{2,1,0:T(2,128)S(1)}, f32[1,2,16384]{2,1,0:T(2,128)S(1)}, u32[]{:S(2)}, u32[]{:S(2)}) %collective-permute-start.13) | collective-permute-done | bytes 131104 | tf_op jit(solution)/shard_map/ppermute | solution.py:27
  113.4 3.3 %collective-permute-done.14 = f32[1,1,16384]{2,1,0:T(1,128)S(1)} collective-permute-done((f32[1,1,16384]{2,1,0:T(1,128)S(1)}, f32[1,1,16384]{2,1,0:T(1,128)S(1)}, u32[]{:S(2)}, u32[]{:S(2)}) %collective-permute-start.14) | collective-permute-done | bytes 65568 | tf_op jit(solution)/shard_map/ppermute | solution.py:27
  116.8 2.7 %collective-permute-done.4 = f32[1,2,16384]{2,1,0:T(2,128)S(1)} collective-permute-done((f32[1,2,16384]{2,1,0:T(2,128)S(1)}, f32[1,2,16384]{2,1,0:T(2,128)S(1)}, u32[]{:S(2)}, u32[]{:S(2)}) %collective-permute-start.4) | collective-permute-done | bytes 131104 | tf_op jit(solution)/shard_map/ppermute | solution.py:18
  119.5 17.2 %all_gather.6 = f32[1,2,65536]{2,1,0:T(2,128)S(1)} all-gather(f32[1,2,16384]{2,1,0:T(2,128)S(1)} %pad_maximum_fusion.1), channel_id=1, replica_groups=mesh['inst'=4,'shard'=8] {'inst'}, dimensions={2}, use_global_device_ids=true | all-gather | bytes 655360 | tf_op jit(solution)/shard_map/all_gather | solution.py:55
  136.8 1.2 collective-permute-start.6
  138.0 16.3 %all_gather.7 = f32[1,2,65536]{2,1,0:T(2,128)S(1)} all-gather(f32[1,2,16384]{2,1,0:T(2,128)S(1)} %pad_maximum_fusion.2), channel_id=1, replica_groups=mesh['inst'=4,'shard'=8] {'inst'}, dimensions={2}, use_global_device_ids=true | all-gather | bytes 655360 | tf_op jit(solution)/shard_map/all_gather | solution.py:56
  154.5 1.1 gather_fusion
  155.6 3.9 %fusion.12 = f32[]{:T(128)} fusion(f32[4,2,16384]{2,1,0:T(2,128)S(1)} %gather_fusion, s32[4,16384]{1,0:T(4,128)S(1)} %multiply_add_fusion, s32[2]{0:T(128)S(1)} %and_select_fusion.4), kind=kLoop, calls=%fused_computation.20 | loop fusion | flops 2490367 | bytes 786444 | tf_op jit(solution)/shard_map/reduce_sum | solution.py:45
  159.5 4.1 %fusion.13 = f32[]{:T(128)} fusion(f32[1,2,65536]{2,1,0:T(2,128)S(1)} %all_gather.7, f32[2,65536]{1,0:T(2,128)S(1)} %bitcast.38, f32[1,2,65536]{2,1,0:T(2,128)S(1)} %all_gather.6, s32[2]{0:T(128)S(1)} %and_select_fusion.4), kind=kLoop, calls=%fused_computation.24 | loop fusion | flops 2752511 | bytes 1572876 | tf_op jit(solution)/shard_map/reduce_sum | solution.py:45
  163.6 1.4 pad_maximum_fusion.3
  165.8 11.8 %psum.31 = f32[2]{0:T(128)S(1)} all-reduce(f32[2]{0:T(128)S(1)} %pad_maximum_fusion.3), channel_id=1, replica_groups=mesh['inst'=4,'shard'=8] {'shard'}, use_global_device_ids=true, to_apply=%region_5.6 | all-reduce | flops 2 | bytes 16 | tf_op jit(solution)/shard_map/psum | solution.py:49
  (58 shorter events, 13.2 us)
Async XLA Ops:
  7.2 76.7 %all-reduce.3.cloned.1.call-start = ((), (), s32[]{:S(2)}) async-start(), calls=%async_computation | async-start | bytes 3145728 | tf_op jit(solution)/shard_map/psum | solution.py:32
  7.2 0.7 copy-start.5
  9.1 2.2 %copy-start.1 = (f32[1,2,65536]{2,1,0:T(2,128)S(1)}, f32[1,2,65536]{2,1,0:T(2,128)}, u32[]{:S(2)}) copy-start(f32[1,2,65536]{2,1,0:T(2,128)} %param.7) | copy-start | bytes 1572868
  9.1 2.2 %copy-start.2 = (f32[1,2,65536]{2,1,0:T(2,128)S(1)}, f32[1,2,65536]{2,1,0:T(2,128)}, u32[]{:S(2)}) copy-start(f32[1,2,65536]{2,1,0:T(2,128)} %param.6) | copy-start | bytes 1572868
  12.8 0.7 copy-start.4
  83.9 3.6 %copy-start.3 = (f32[1,2,65536]{2,1,0:T(2,128)S(1)}, f32[1,2,65536]{2,1,0:T(2,128)}, u32[]{:S(2)}) copy-start(f32[1,2,65536]{2,1,0:T(2,128)} %get-tuple-element.7) | copy-start | bytes 1572868
  84.9 5.3 %collective-permute-start = (f32[1,2,16384]{2,1,0:T(2,128)S(1)}, f32[1,2,16384]{2,1,0:T(2,128)S(1)}, u32[]{:S(2)}, u32[]{:S(2)}) collective-permute-start(f32[1,2,16384]{2,1,0:T(2,128)S(1)} %constant_dynamic-slice_fusion.2), channel_id=1, source_target_pairs={{0,1},{1,2},{2,3},{3,4},{4,5},{5,6},{6,7},{7,0},{8,9},{9,10},{10,1... | collective-permute-start | bytes 393224 | tf_op jit(solution)/shard_map/ppermute | solution.py:27
  85.8 6.0 %collective-permute-start.7 = (f32[1,2,16384]{2,1,0:T(2,128)S(1)}, f32[1,2,16384]{2,1,0:T(2,128)S(1)}, u32[]{:S(2)}, u32[]{:S(2)}) collective-permute-start(f32[1,2,16384]{2,1,0:T(2,128)S(1)} %constant_dynamic-slice_fusion.1), channel_id=1, source_target_pairs={{0,1},{1,2},{2,3},{3,4},{4,5},{5,6},{6,7},{7,0},{8,9},{9,10},{10,1... | collective-permute-start | bytes 393224 | tf_op jit(solution)/shard_map/ppermute | solution.py:27
  87.5 7.7 %collective-permute-start.11 = (f32[1,2,16384]{2,1,0:T(2,128)S(1)}, f32[1,2,16384]{2,1,0:T(2,128)S(1)}, u32[]{:S(2)}, u32[]{:S(2)}) collective-permute-start(f32[1,2,16384]{2,1,0:T(2,128)S(1)} %constant_dynamic-slice_fusion), channel_id=1, source_target_pairs={{0,1},{1,2},{2,3},{3,4},{4,5},{5,6},{6,7},{7,0},{8,9},{9,10},{10,1... | collective-permute-start | bytes 393224 | tf_op jit(solution)/shard_map/ppermute | solution.py:27
  91.2 7.2 %collective-permute-start.1 = (f32[1,2,16384]{2,1,0:T(2,128)S(1)}, f32[1,2,16384]{2,1,0:T(2,128)S(1)}, u32[]{:S(2)}, u32[]{:S(2)}) collective-permute-start(f32[1,2,16384]{2,1,0:T(2,128)S(1)} %broadcast_select_fusion.5), channel_id=1, source_target_pairs={{0,2},{1,3},{2,4},{3,5},{4,6},{5,7},{6,0},{7,1},{8,10},{9,11},{10,... | collective-permute-start | bytes 393224 | tf_op jit(solution)/shard_map/ppermute | solution.py:27
  92.8 8.5 %collective-permute-start.8 = (f32[1,2,16384]{2,1,0:T(2,128)S(1)}, f32[1,2,16384]{2,1,0:T(2,128)S(1)}, u32[]{:S(2)}, u32[]{:S(2)}) collective-permute-start(f32[1,2,16384]{2,1,0:T(2,128)S(1)} %broadcast_select_fusion.4), channel_id=1, source_target_pairs={{0,2},{1,3},{2,4},{3,5},{4,6},{5,7},{6,0},{7,1},{8,10},{9,11},{10,... | collective-permute-start | bytes 393224 | tf_op jit(solution)/shard_map/ppermute | solution.py:27
  95.3 7.5 %collective-permute-start.12 = (f32[1,2,16384]{2,1,0:T(2,128)S(1)}, f32[1,2,16384]{2,1,0:T(2,128)S(1)}, u32[]{:S(2)}, u32[]{:S(2)}) collective-permute-start(f32[1,2,16384]{2,1,0:T(2,128)S(1)} %broadcast_select_fusion.3), channel_id=1, source_target_pairs={{0,2},{1,3},{2,4},{3,5},{4,6},{5,7},{6,0},{7,1},{8,10},{9,11},{10,... | collective-permute-start | bytes 393224 | tf_op jit(solution)/shard_map/ppermute | solution.py:27
  98.5 7.1 %collective-permute-start.2 = (f32[1,2,16384]{2,1,0:T(2,128)S(1)}, f32[1,2,16384]{2,1,0:T(2,128)S(1)}, u32[]{:S(2)}, u32[]{:S(2)}) collective-permute-start(f32[1,2,16384]{2,1,0:T(2,128)S(1)} %broadcast_select_fusion.8), channel_id=1, source_target_pairs={{0,4},{1,5},{2,6},{3,7},{4,0},{5,1},{6,2},{7,3},{8,12},{9,13},{10,... | collective-permute-start | bytes 393224 | tf_op jit(solution)/shard_map/ppermute | solution.py:27
  101.3 7.1 %collective-permute-start.9 = (f32[1,2,16384]{2,1,0:T(2,128)S(1)}, f32[1,2,16384]{2,1,0:T(2,128)S(1)}, u32[]{:S(2)}, u32[]{:S(2)}) collective-permute-start(f32[1,2,16384]{2,1,0:T(2,128)S(1)} %broadcast_select_fusion.7), channel_id=1, source_target_pairs={{0,4},{1,5},{2,6},{3,7},{4,0},{5,1},{6,2},{7,3},{8,12},{9,13},{10,... | collective-permute-start | bytes 393224 | tf_op jit(solution)/shard_map/ppermute | solution.py:27
  102.9 9.0 %collective-permute-start.13 = (f32[1,2,16384]{2,1,0:T(2,128)S(1)}, f32[1,2,16384]{2,1,0:T(2,128)S(1)}, u32[]{:S(2)}, u32[]{:S(2)}) collective-permute-start(f32[1,2,16384]{2,1,0:T(2,128)S(1)} %broadcast_select_fusion.6), channel_id=1, source_target_pairs={{0,4},{1,5},{2,6},{3,7},{4,0},{5,1},{6,2},{7,3},{8,12},{9,13},{10,... | collective-permute-start | bytes 393224 | tf_op jit(solution)/shard_map/ppermute | solution.py:27
  105.8 6.3 %collective-permute-start.3 = (f32[1,1,16384]{2,1,0:T(1,128)S(1)}, f32[1,1,16384]{2,1,0:T(1,128)S(1)}, u32[]{:S(2)}, u32[]{:S(2)}) collective-permute-start(f32[1,1,16384]{2,1,0:T(1,128)S(1)} %get-tuple-element.14), channel_id=1, source_target_pairs={{0,1},{1,2},{2,3},{3,4},{4,5},{5,6},{6,7},{7,0},{8,9},{9,10},{10,1... | collective-permute-start | bytes 196616 | tf_op jit(solution)/shard_map/ppermute | solution.py:27
  108.6 4.6 %collective-permute-start.10 = (f32[1,1,16384]{2,1,0:T(1,128)S(1)}, f32[1,1,16384]{2,1,0:T(1,128)S(1)}, u32[]{:S(2)}, u32[]{:S(2)}) collective-permute-start(f32[1,1,16384]{2,1,0:T(1,128)S(1)} %get-tuple-element.10), channel_id=1, source_target_pairs={{0,1},{1,2},{2,3},{3,4},{4,5},{5,6},{6,7},{7,0},{8,9},{9,10},{10,1... | collective-permute-start | bytes 196616 | tf_op jit(solution)/shard_map/ppermute | solution.py:27
  112.0 4.6 %collective-permute-start.14 = (f32[1,1,16384]{2,1,0:T(1,128)S(1)}, f32[1,1,16384]{2,1,0:T(1,128)S(1)}, u32[]{:S(2)}, u32[]{:S(2)}) collective-permute-start(f32[1,1,16384]{2,1,0:T(1,128)S(1)} %get-tuple-element.8), channel_id=1, source_target_pairs={{0,1},{1,2},{2,3},{3,4},{4,5},{5,6},{6,7},{7,0},{8,9},{9,10},{10,1... | collective-permute-start | bytes 196616 | tf_op jit(solution)/shard_map/ppermute | solution.py:27
  112.3 7.3 %collective-permute-start.4 = (f32[1,2,16384]{2,1,0:T(2,128)S(1)}, f32[1,2,16384]{2,1,0:T(2,128)S(1)}, u32[]{:S(2)}, u32[]{:S(2)}) collective-permute-start(f32[1,2,16384]{2,1,0:T(2,128)S(1)} %get-tuple-element.13), channel_id=1, source_target_pairs={{0,8},{8,16},{16,24},{24,0},{1,9},{9,17},{17,25},{25,1},{2,10},{10... | collective-permute-start | bytes 393224 | tf_op jit(solution)/shard_map/ppermute | solution.py:18
  119.5 17.2 %collective-permute-start.5 = (f32[1,2,16384]{2,1,0:T(2,128)S(1)}, f32[1,2,16384]{2,1,0:T(2,128)S(1)}, u32[]{:S(2)}, u32[]{:S(2)}) collective-permute-start(f32[1,2,16384]{2,1,0:T(2,128)S(1)} %collective-permute-done.4), channel_id=1, source_target_pairs={{0,8},{8,16},{16,24},{24,0},{1,9},{9,17},{17,25},{25,1},{2,10},{10... | collective-permute-start | bytes 393224 | tf_op jit(solution)/shard_map/ppermute | solution.py:18
  136.8 17.5 %collective-permute-start.6 = (f32[1,2,16384]{2,1,0:T(2,128)S(1)}, f32[1,2,16384]{2,1,0:T(2,128)S(1)}, u32[]{:S(2)}, u32[]{:S(2)}) collective-permute-start(f32[1,2,16384]{2,1,0:T(2,128)S(1)} %collective-permute-done.5), channel_id=1, source_target_pairs={{0,8},{8,16},{16,24},{24,0},{1,9},{9,17},{17,25},{25,1},{2,10},{10... | collective-permute-start | bytes 393224 | tf_op jit(solution)/shard_map/ppermute | solution.py:18
  155.6 9.4 %copy-start = (f32[4,2,16384]{2,1,0:T(2,128)}, f32[4,2,16384]{2,1,0:T(2,128)S(1)}, u32[]{:S(2)}) copy-start(f32[4,2,16384]{2,1,0:T(2,128)S(1)} %gather_fusion) | copy-start | bytes 1572868
Sparse Core Ops, SparseCore 0:
  12.9 70.8 all-reduce.2
